TPU v7x, 512 devices: a whole 4x8x8 slice. The times are simulated.
512 devices in a mesh: scen: 8 (over y), blk: 64 (over z, x, core).
Axes of the slice: x: 4, y: 8, z: 8, core: 2. Of those that a mesh axis runs over, the one named last changes fastest.
Arguments:
- returns: bfloat16 [512, 32768], P(('scen', 'blk')), may hold values from -6 to 6
- vol_hist: float32 [512, 32768], P(('scen', 'blk')), may hold values from 0.5 to 5.5, as said below
- vol_now: float32 [32768], replicated, may hold values from 0.5 to 2
- sensitivity: bfloat16 [16384, 128, 128], P('blk'), may hold values from -0.109375 to 0.109375
- block_pairs: int32 [16384, 3], P('blk'), may hold values from 0 to 255, as said below
- book_order: int32 [128], replicated, may hold values from 0 to 127, each once
Outputs:
- profit_loss: float32 [512, 16384], P('scen', 'blk')
- book_rms: float32 [16384], P('blk')
Inputs may be any that keep to these rules, and one draw needn't show every extreme that they name: `block_pairs`: each index k of blk holds 256 slots; their factor blocks lie in k * 4 to k * 4 + 3; on each index the live slots come first; some index has all 256 slots live. `vol_hist`: positive volatilities.
All inputs are finite; a program needn't handle non-finite values.
Results may differ from a plain program's by a relative error of at most 0.0029.
Values may be sent and summed in bfloat16 or wider, within the bound.
A program may use at most 64 MiB of HBM per device.

v0:
```python
import jax
import jax.numpy as jnp
from jax import lax
from jax.sharding import PartitionSpec as P


def shards(returns, vol_hist, vol_now, sensitivity, block_pairs, book_order):
    rescaled = (returns.astype(jnp.float32) * vol_now[None, :] / vol_hist).astype(jnp.bfloat16)
    groups = lax.axis_size("blk")
    column = lax.axis_index("blk")
    block_size = sensitivity.shape[1]
    own_width = rescaled.shape[1] // groups
    gathered = lax.all_gather(rescaled, "blk", axis=0, tiled=True)
    own_shocks = lax.dynamic_slice_in_dim(gathered, column * own_width, own_width, 1)
    scen_rows = own_shocks.shape[0]
    local_blocks = own_shocks.reshape(scen_rows, own_width // block_size, block_size)
    factor_local = block_pairs[:, 0] - column * (own_width // block_size)
    picked = jnp.take(local_blocks, factor_local, axis=1)
    products = jnp.einsum("skc,kcd->ksd", picked, sensitivity, preferred_element_type=jnp.float32)
    book_blocks = book_order.shape[0]
    matches = book_order[None, :] == block_pairs[:, 1][:, None]
    position = jnp.sum(
        jnp.where(matches, jnp.arange(book_blocks, dtype=jnp.int32)[None, :], 0), axis=1
    )
    live_weight = block_pairs[:, 2].astype(jnp.float32)
    selector = jnp.where(
        jnp.arange(book_blocks, dtype=jnp.int32)[:, None] == position[None, :],
        live_weight[None, :],
        0.0,
    )
    partial_sum = jnp.einsum("bk,ksd->bsd", selector, products, precision=lax.Precision.HIGHEST)
    owned_books = lax.psum_scatter(partial_sum, "blk", scatter_dimension=0, tiled=True)
    profit_loss = owned_books.transpose(1, 0, 2).reshape(scen_rows, -1)
    squares = lax.psum(jnp.sum(profit_loss * profit_loss, axis=0), "scen")
    total_rows = scen_rows * lax.axis_size("scen")
    book_rms = jnp.sqrt(squares / total_rows + 1e-06)
    return (profit_loss, book_rms)


def solution(mesh):
    return jax.shard_map(
        shards,
        mesh=mesh,
        in_specs=(
            P(("scen", "blk"), None),
            P(("scen", "blk"), None),
            P(),
            P("blk", None, None),
            P("blk", None),
            P(),
        ),
        out_specs=(P("scen", "blk"), P("blk")),
        check_vma=False,
    )
```

profile of v0, /device:TPU:2, one launch (start us, length us, event | category | flops | bytes accessed | tf_op | source)
XLA Modules:
  0.0 306.9 jit_solution(5500297832278596794)
XLA Ops:
  7.2 0.0 all-gather.3.cloned.1.call-start
  7.2 1.9 convert_bitcast_fusion
  9.1 0.0 all-gather.3.cloned.1.call-update
  9.1 0.0 reduce-scatter.2.cloned.1.call-start
  9.2 0.7 and_reduce_fusion
  9.9 0.8 fusion.15
  10.7 0.8 select_reduce_fusion
  11.5 93.0 %all-gather.3.cloned.1.call-done = bf16[64,1,32768]{2,1,0:T(2,128)(2,1)} async-done(((bf16[1,1,32768]{2,1,0:T(2,128)(2,1)}), bf16[64,1,32768]{2,1,0:T(2,128)(2,1)}) %all-gather.3.cloned.1.call-update) | async-done | bytes 4194320 | tf_op jit(solution)/shard_map/all_gather | solution.py:13
  104.5 1.3 dynamic-slice_reduce_fusion
  105.8 3.0 gather_fusion
  108.8 7.0 %fusion.2 = f32[256,64,128]{2,1,0:T(8,128)S(1)} fusion(bf16[256,128,128]{2,1,0:T(8,128)(2,1)} %param.9, bf16[256,64,128]{2,1,0:T(8,128)(2,1)} %gather_fusion, pred[256]{0:T(512)(128)(4,1)S(1)} %get-tuple-element.2), kind=kOutput, calls=%fused_computation.3 | convolution fusion | flops 538968064 | bytes 20971776 | tf_op jit(solution)/shard_map/skc,kcd->ksd/dot_general | solution.py:19
  115.9 10.2 %fusion = f32[128,64,128]{2,0,1:T(8,128)S(1)} fusion(f32[256,64,128]{2,1,0:T(8,128)S(1)} %fusion.2, f32[256]{0:T(256)S(1)} %bitcast.32, s32[256]{0:T(256)S(1)} %select_reduce_fusion), kind=kOutput, calls=%fused_computation.1 | convolution fusion | flops 3221291008 | bytes 12584960 | tf_op jit(solution)/shard_map/bk,ksd->bsd/dot_general | solution.py:31
  126.1 4.4 %copy.18 = f32[128,64,128]{2,1,0:T(8,128)} copy(f32[128,64,128]{2,0,1:T(8,128)S(1)} %fusion) | data formatting | bytes 8388608 | tf_op jit(solution)/shard_map/bk,ksd->bsd/dot_general | solution.py:31
  130.4 0.0 reduce-scatter.2.cloned.1.call-update
  130.5 149.7 %reduce-scatter.2.cloned.1.call-done = f32[2,64,128]{2,1,0:T(8,128)} async-done(((f32[128,64,128]{2,1,0:T(8,128)}), f32[2,64,128]{2,1,0:T(8,128)}) %reduce-scatter.2.cloned.1.call-update) | async-done | bytes 65552 | tf_op jit(solution)/shard_map/reduce_scatter | solution.py:32
  280.2 0.9 fusion.9
  281.1 17.0 %psum.7 = f32[256]{0:T(256)S(1)} all-reduce(f32[256]{0:T(256)S(1)} %bitcast.29), channel_id=1, replica_groups=mesh['scen'=8,'blk'=64] {'scen'}, use_global_device_ids=true, to_apply=%region_3.4 | all-reduce | flops 256 | bytes 2048 | tf_op jit(solution)/shard_map/psum | solution.py:34
  298.0 0.6 add_sqrt_fusion
  298.6 1.5 copy_bitcast_fusion
  (2 shorter events, 0.0 us)
Async XLA Ops:
  7.2 97.4 %all-gather.3.cloned.1.call-start = ((), (), s32[]{:S(2)}) async-start(), calls=%async_computation.2 | async-start | bytes 8519680 | tf_op jit(solution)/shard_map/all_gather | solution.py:13
  9.1 271.0 %reduce-scatter.2.cloned.1.call-start = ((), (), s32[]{:S(2)}) async-start(), calls=%async_computation.1 | async-start | bytes 4259840 | tf_op jit(solution)/shard_map/reduce_scatter | solution.py:32
Sparse Core Ops, SparseCore 0:
  11.3 93.1 all-gather.2
  130.6 149.5 reduce-scatter.1
where the time goes:
time: 307 us
  waiting for transfers between devices  243 us (79%)
  matrix products  17.2 us (6%)
  blocking collectives  17 us (6%)
  between operations  14.1 us (5%)
  local copies, waits for them, and re-layouts  10.1 us (3%)
  other arithmetic  5.67 us (2%)
    reduce_scatter x1, waiting for transfers between devices, shards(): lax.psum_scatter(partial_sum, 'blk', scatter_dimension=0, tiled=True)  150 us
    all_gather x1, waiting for transfers between devices, shards(): gathered = lax.all_gather(rescaled, 'blk', axis=0, tiled=True)  93 us
    psum x1, blocking collectives, shards(): squares = lax.psum(jnp.sum(profit_loss * profit_loss, axis=0), 'scen')  17 us
    dot_general x1, matrix products, shards(): jnp.einsum('bk,ksd->bsd', selector, products, precision=lax.Precision.HIG...  10.2 us
    dot_general x1, matrix products, shards(): jnp.einsum('skc,kcd->ksd', picked, sensitivity, preferred_element_type=jn...  7.02 us
  transfers between devices with their start and end apart: 2, of which 2 were waited for; matrix products, arithmetic and copies ran while one was open for 1% of the time, Pallas kernels for 0%

commit v1 on v0

--- a/solution.py
+++ b/solution.py
@@ -10,7 +10,10 @@
     column = lax.axis_index("blk")
     block_size = sensitivity.shape[1]
     own_width = rescaled.shape[1] // groups
-    gathered = lax.all_gather(rescaled, "blk", axis=0, tiled=True)
+    back = lax.axis_size("blk")
+    arr_out = jnp.stack([rescaled] * back)
+    item_now = lax.all_to_all(arr_out, axis_name="blk", split_axis=0, concat_axis=0)
+    gathered = jnp.concatenate(item_now, axis=0)
     own_shocks = lax.dynamic_slice_in_dim(gathered, column * own_width, own_width, 1)
     scen_rows = own_shocks.shape[0]
     local_blocks = own_shocks.reshape(scen_rows, own_width // block_size, block_size)

time: 307 us -> 382 us (1.24)
  local copies, waits for them, and re-layouts: 10.1 us -> 43.9 us
  other arithmetic: 5.67 us -> 29.9 us
  starting transfers between devices: 0.08 us -> 14.2 us
    all_to_all x0 -> x1, waiting for transfers between devices: none -> 95.8 us  [shards(): lax.all_to_all(arr_out, axis_name='blk', split_axis=0, concat_axis=0)]
    all_gather x1 -> x0, waiting for transfers between devices: 93 us -> none  [shards(): gathered = lax.all_gather(rescaled, 'blk', axis=0, tiled=True)]
    unnamed x0 -> x6, local copies, waits for them, and re-layouts: none -> 27.6 us
    another operation x0 -> x1, other arithmetic: none -> 26.7 us  [shards(): arr_out = jnp.stack([rescaled] * back)]
    all_to_all x0 -> x1, starting transfers between devices: none -> 14.2 us  [shards(): lax.all_to_all(arr_out, axis_name='blk', split_axis=0, concat_axis=0)]
    another operation x0 -> x2, local copies, waits for them, and re-layouts: none -> 6.13 us  [shards(): arr_out = jnp.stack([rescaled] * back)]
  transfers between devices with their start and end apart: 2 -> 2, of which waited for: 2 -> 2; matrix products, arithmetic and copies ran while one was open for 1% -> 0% of each run, Pallas kernels for 0% -> 0%
where the time goes in v1:
time: 382 us; the launch traced here: 381 us
  waiting for transfers between devices  244 us (64%)
  local copies, waits for them, and re-layouts  43.9 us (11%)
  other arithmetic  29.9 us (8%)
  matrix products  17.3 us (5%)
  blocking collectives  16.9 us (4%)
  starting transfers between devices  14.2 us (4%)
  between operations  14.1 us (4%)
    reduce_scatter x1, waiting for transfers between devices, shards(): lax.psum_scatter(partial_sum, 'blk', scatter_dimension=0, tiled=True)  148 us
    all_to_all x1, waiting for transfers between devices, shards(): lax.all_to_all(arr_out, axis_name='blk', split_axis=0, concat_axis=0)  95.8 us
    unnamed x6, local copies, waits for them, and re-layouts  27.6 us
    another operation x1, other arithmetic, shards(): arr_out = jnp.stack([rescaled] * back)  26.7 us
    psum x1, blocking collectives, shards(): squares = lax.psum(jnp.sum(profit_loss * profit_loss, axis=0), 'scen')  16.9 us
    all_to_all x1, starting transfers between devices, shards(): lax.all_to_all(arr_out, axis_name='blk', split_axis=0, concat_axis=0)  14.2 us
    dot_general x1, matrix products, shards(): jnp.einsum('bk,ksd->bsd', selector, products, precision=lax.Precision.HIG...  10.3 us
  transfers between devices with their start and end apart: 2, of which 2 were waited for; matrix products, arithmetic and copies ran while one was open for 0% of the time, Pallas kernels for 0%

profile of v1, /device:TPU:2, one launch (start us, length us, event | category | flops | bytes accessed | tf_op | source)
XLA Modules:
  0.0 380.6 jit_solution(13877792165904643910)
XLA Ops:
  7.2 1.5 convert_reduce_fusion
  8.7 5.6 %stack.2 = bf16[64,1,32768]{2,1,0:T(2,128)(2,1)} broadcast(bf16[32768]{0:T(1024)(128)(2,1)S(1)} %convert_reduce_fusion), dimensions={2} | broadcast | bytes 4259840 | tf_op jit(solution)/shard_map/stack | solution.py:14
  14.3 0.5 broadcast.34
  14.8 26.7 %reduce.7 = bf16[64,32768]{1,0:T(8,128)(2,1)} reduce(bf16[64,1,32768]{2,1,0:T(2,128)(2,1)} %stack.2, bf16[]{:T(256)} %broadcast.34), dimensions={1}, to_apply=%stack.2.reduce_sub_computation | reduce | bytes 8388610 | tf_op jit(solution)/shard_map/stack | solution.py:14
  41.5 7.8 %reshape.43 = bf16[64,2,16384]{2,1,0:T(2,128)(2,1)} reshape(bf16[64,32768]{1,0:T(8,128)(2,1)} %reduce.7) | data formatting | bytes 8388608
  49.3 0.0 copy-start
  49.3 0.0 copy-start.1
  49.3 14.2 %all-to-all-start = ((bf16[64,2,16384]{2,1,0:T(2,128)(2,1)}), bf16[64,2,16384]{2,1,0:T(2,128)(2,1)}, u32[]{:S(2)}, u32[]{:S(2)}) async-start(bf16[64,2,16384]{2,1,0:T(2,128)(2,1)} %reshape.43), calls=%async_computation | async-start | bytes 8388608 | tf_op jit(solution)/shard_map/all_to_all | solution.py:15
  63.5 0.0 reduce-scatter.2.cloned.1.call-start
  63.6 0.0 copy-done
  63.6 0.0 copy-done.1
  63.6 0.2 select_reduce_fusion
  63.8 95.8 %all-to-all-done = bf16[64,2,16384]{2,1,0:T(2,128)(2,1)} async-done(((bf16[64,2,16384]{2,1,0:T(2,128)(2,1)}), bf16[64,2,16384]{2,1,0:T(2,128)(2,1)}, u32[]{:S(2)}, u32[]{:S(2)}) %all-to-all-start) | async-done | bytes 4194336 | tf_op jit(solution)/shard_map/all_to_all | solution.py:15
  159.6 19.8 %reshape.44 = bf16[64,1,32768]{2,1,0:T(2,128)(2,1)} reshape(bf16[64,2,16384]{2,1,0:T(2,128)(2,1)} %all-to-all-done) | data formatting | bytes 8388608
  179.4 1.3 dynamic-slice_reduce_fusion
  180.7 3.0 gather_fusion
  183.7 7.0 %fusion.2 = f32[256,64,128]{2,1,0:T(8,128)S(1)} fusion(bf16[256,128,128]{2,1,0:T(8,128)(2,1)} %param.9, bf16[256,64,128]{2,1,0:T(8,128)(2,1)} %gather_fusion, pred[256]{0:T(512)(128)(4,1)S(1)} %get-tuple-element.2), kind=kOutput, calls=%fused_computation.3 | convolution fusion | flops 538968064 | bytes 20971776 | tf_op jit(solution)/shard_map/skc,kcd->ksd/dot_general | solution.py:22
  190.8 10.3 %fusion = f32[128,64,128]{2,0,1:T(8,128)S(1)} fusion(f32[256,64,128]{2,1,0:T(8,128)S(1)} %fusion.2, f32[256]{0:T(256)S(1)} %bitcast.30, s32[256]{0:T(256)S(1)} %select_reduce_fusion), kind=kOutput, calls=%fused_computation.1 | convolution fusion | flops 3221291008 | bytes 12584960 | tf_op jit(solution)/shard_map/bk,ksd->bsd/dot_general | solution.py:34
  201.0 4.4 %copy.18 = f32[128,64,128]{2,1,0:T(8,128)} copy(f32[128,64,128]{2,0,1:T(8,128)S(1)} %fusion) | data formatting | bytes 8388608 | tf_op jit(solution)/shard_map/bk,ksd->bsd/dot_general | solution.py:34
  205.4 0.0 reduce-scatter.2.cloned.1.call-update
  205.4 148.5 %reduce-scatter.2.cloned.1.call-done = f32[2,64,128]{2,1,0:T(8,128)} async-done(((f32[128,64,128]{2,1,0:T(8,128)}), f32[2,64,128]{2,1,0:T(8,128)}) %reduce-scatter.2.cloned.1.call-update) | async-done | bytes 65552 | tf_op jit(solution)/shard_map/reduce_scatter | solution.py:35
  353.9 0.9 fusion.9
  354.8 16.9 %psum.7 = f32[256]{0:T(256)S(1)} all-reduce(f32[256]{0:T(256)S(1)} %bitcast.27), channel_id=1, replica_groups=mesh['scen'=8,'blk'=64] {'scen'}, use_global_device_ids=true, to_apply=%region_3.4 | all-reduce | flops 256 | bytes 2048 | tf_op jit(solution)/shard_map/psum | solution.py:37
  371.7 0.6 add_sqrt_fusion
  372.2 1.5 copy_bitcast_fusion
  (4 shorter events, 0.0 us)
Async XLA Ops:
  49.3 14.3 %copy-start = (s32[256,3]{0,1:T(4,128)S(1)}, s32[256,3]{0,1:T(4,128)}, u32[]{:S(2)}) copy-start(s32[256,3]{0,1:T(4,128)} %param.10) | copy-start | bytes 9220
  49.3 14.3 %copy-start.1 = (s32[128]{0:T(128)S(1)}, s32[128]{0:T(128)}, u32[]{:S(2)}) copy-start(s32[128]{0:T(128)} %param.11) | copy-start | bytes 1540
  49.3 110.3 %all-to-all-start = ((bf16[64,2,16384]{2,1,0:T(2,128)(2,1)}), bf16[64,2,16384]{2,1,0:T(2,128)(2,1)}, u32[]{:S(2)}, u32[]{:S(2)}) async-start(bf16[64,2,16384]{2,1,0:T(2,128)(2,1)} %reshape.43), calls=%async_computation | async-start | bytes 8388608 | tf_op jit(solution)/shard_map/all_to_all | solution.py:15
  63.5 290.4 %reduce-scatter.2.cloned.1.call-start = ((), (), s32[]{:S(2)}) async-start(), calls=%async_computation.2 | async-start | bytes 4259840 | tf_op jit(solution)/shard_map/reduce_scatter | solution.py:35
Sparse Core Ops, SparseCore 0:
  205.5 148.3 reduce-scatter.1
